TPU v7x, 256 devices: a whole 4x4x8 slice. The times are simulated.
256 devices in a mesh: pipe: 16 (over y_hi, z), vocab: 16 (over y_lo, x, core).
Axes of the slice: x: 4, y: 4 (y_hi: 2, y_lo: 2; y = y_hi * 2 + y_lo), z: 8, core: 2. Of those that a mesh axis runs over, the one named last changes fastest.
Arguments:
- final_hidden: bfloat16 [512, 4608], P('pipe', 'vocab'), may hold values from -6 to 6
- tied_table: bfloat16 [163840, 4608], P(('pipe', 'vocab')), may hold values from -1.2 to 1.2
- target_ids: int32 [512], replicated, may hold values from 0 to 163839
- input_ids: int32 [512], replicated, may hold values from 0 to 163839
- embed_cot: bfloat16 [512, 4608], P('pipe', 'vocab'), may hold values from -0.3125 to 0.3125
Outputs:
- grad_table: bfloat16 [163840, 4608], P(('pipe', 'vocab'))
- grad_hidden: float32 [512, 4608], P('pipe', 'vocab')
- token_loss: float32 [512], P('pipe')
All inputs are finite; a program needn't handle non-finite values.
Results may differ from a plain program's by a relative error of at most 0.01.
Values may be sent and summed in bfloat16 or wider, within the bound.
A program may use at most 128 MiB of HBM per device.

v0:
```python
import jax
import jax.numpy as jnp
from jax import lax
from jax.sharding import PartitionSpec as P

D = 4608


def local(final_hidden, tied_table, target_ids, input_ids, embed_cot):
    whole_h, whole_c = (
        lax.all_gather(final_hidden, "vocab", axis=1, tiled=True),
        lax.all_gather(embed_cot, "vocab", axis=1, tiled=True),
    )
    whole_h, whole_c = (
        lax.all_gather(whole_h, "pipe", axis=0, tiled=True),
        lax.all_gather(whole_c, "pipe", axis=0, tiled=True),
    )
    rows_dev = tied_table.shape[0]
    offset = lax.axis_index(("pipe", "vocab")) * rows_dev
    vocab_ids = offset + jnp.arange(rows_dev, dtype=jnp.int32)
    logits = jnp.einsum("td,vd->tv", whole_h, tied_table, preferred_element_type=jnp.float32)
    tanh_part = jnp.tanh(logits / 30.0)
    capped = 30.0 * tanh_part
    exponent = jnp.exp(capped)
    target_mask = vocab_ids[None, :] == target_ids[:, None]
    local_sum = jnp.sum(exponent, axis=1)
    local_target = jnp.sum(jnp.where(target_mask, capped, 0.0), axis=1)
    sum_exp, target_logit = lax.psum((local_sum, local_target), ("pipe", "vocab"))
    token_loss = jnp.log(sum_exp) - target_logit
    dlogits = (
        (exponent / sum_exp[:, None] - target_mask.astype(jnp.float32))
        * (1.0 - tanh_part * tanh_part)
    ).astype(jnp.bfloat16)
    head_grad = jnp.einsum("tv,td->vd", dlogits, whole_h, preferred_element_type=jnp.float32)
    input_mask = (vocab_ids[:, None] == input_ids[None, :]).astype(jnp.bfloat16)
    embed_grad = jnp.dot(input_mask, whole_c, preferred_element_type=jnp.float32)
    grad_table = (head_grad + float(D) ** 0.5 * embed_grad).astype(jnp.bfloat16)
    products = jnp.dot(dlogits, tied_table, preferred_element_type=jnp.float32)
    partial_value = lax.psum_scatter(
        products.astype(jnp.bfloat16), "vocab", scatter_dimension=1, tiled=True
    ).astype(jnp.float32)
    grad_hidden = lax.psum_scatter(partial_value, "pipe", scatter_dimension=0, tiled=True)
    held = final_hidden.shape[0]
    loss_shard = lax.dynamic_slice_in_dim(token_loss, lax.axis_index("pipe") * held, held)
    return (grad_table, grad_hidden, loss_shard)


def solution(mesh):
    placed = (P("pipe", "vocab"), P(("pipe", "vocab"), None), P(), P(), P("pipe", "vocab"))
    return jax.shard_map(
        local,
        mesh=mesh,
        in_specs=placed,
        out_specs=(P(("pipe", "vocab"), None), P("pipe", "vocab"), P("pipe")),
        check_vma=False,
    )
```

profile of v0, /device:TPU:2, one launch (start us, length us, event | category | flops | bytes accessed | tf_op | source)
XLA Modules:
  0.0 609.2 jit_solution(8618035419654364876)
XLA Ops:
  7.2 0.0 copy-start
  7.2 0.0 all-gather.5.cloned.1.call-start
  7.2 19.4 %all-gather = bf16[16,288,32]{1,2,0:T(8,128)(2,1)S(1)} all-gather(bf16[1,288,32]{1,2,0:T(8,128)(2,1)} %bitcast.20), channel_id=1, replica_groups=mesh['pipe'=16,'vocab'=16] {'vocab'}, dimensions={0}, use_global_device_ids=true | all-gather | bytes 313344 | tf_op jit(solution)/shard_map/all_gather | solution.py:11
  26.7 0.1 copy.12
  26.8 1.1 reshape.18
  27.9 0.0 all-gather.5.cloned.1.call-update
  27.9 0.0 reduce-scatter.5.cloned.1.call-start
  28.0 105.3 %all-gather.5.cloned.1.call-done = bf16[512,4608]{1,0:T(8,128)(2,1)} async-done(((bf16[32,4608]{1,0:T(8,128)(2,1)}), bf16[512,4608]{1,0:T(8,128)(2,1)}) %all-gather.5.cloned.1.call-update) | async-done | bytes 4718608 | tf_op jit(solution)/shard_map/all_gather | solution.py:15
  133.3 0.0 copy-done
  133.3 7.8 %fusion.4 = (f32[512]{0:T(512)S(1)}, f32[512]{0:T(512)S(1)}, f32[512,640]{1,0:T(8,128)S(1)}) fusion(s32[640]{0:T(1024)S(1)} %iota_add_fusion, s32[512]{0:T(512)S(1)} %copy-done, bf16[512,4608]{1,0:T(8,128)(2,1)} %all-gather.5.cloned.1.call-done, bf16[640,4608]{1,0:T(8,128)(2,1)} %param.6), kind=kOutput, calls=%fused_computation.9 | convolution fusion | flops 3021863936 | bytes 11936256 | tf_op jit(solution)/shard_map/td,vd->tv/dot_general | solution.py:21
  141.0 72.8 %all-reduce = (f32[512]{0:T(512)S(1)}, f32[512]{0:T(512)S(1)}) all-reduce(f32[512]{0:T(512)S(1)} %get-tuple-element.13, f32[512]{0:T(512)S(1)} %get-tuple-element.12), channel_id=1, replica_groups=mesh['pipe'=16,'vocab'=16] {'pipe','vocab'}, use_global_device_ids=true, to_apply=%region_1.2 | all-reduce | flops 1024 | bytes 8192 | tf_op jit(solution)/shard_map/psum | solution.py:28
  213.8 9.8 %convolution_convert_fusion = bf16[512,4608]{0,1:T(8,128)(2,1)} fusion(bf16[640,4608]{1,0:T(8,128)(2,1)} %param.6, f32[512,640]{1,0:T(8,128)S(1)} %get-tuple-element.16, s32[640]{0:T(1024)S(1)} %iota_add_fusion, f32[512]{0:T(512)S(1)} %get-tuple-element.14, s32[512]{0:T(512)S(1)} %copy-done), kind=kOutput, calls=%fused_computation.1 | convolution fusion | flops 3025207296 | bytes 11934208 | tf_op jit(solution)/shard_map/dot_general | solution.py:38
  223.6 0.0 copy-start.1
  223.6 0.0 reduce-scatter.5.cloned.1.call-update
  223.6 0.0 all-gather.7.cloned.1.call-start
  223.7 0.7 copy-done.1
  224.4 19.9 %all-gather.1 = bf16[16,288,32]{1,2,0:T(8,128)(2,1)S(1)} all-gather(bf16[1,288,32]{1,2,0:T(8,128)(2,1)S(1)} %bitcast.21), channel_id=1, replica_groups=mesh['pipe'=16,'vocab'=16] {'vocab'}, dimensions={0}, use_global_device_ids=true | all-gather | bytes 313344 | tf_op jit(solution)/shard_map/all_gather | solution.py:12
  244.3 0.1 copy.13
  244.4 1.1 reshape.20
  245.5 0.0 all-gather.7.cloned.1.call-update
  245.6 0.2 reduce-scatter.7.cloned.1.call-start
  245.8 10.2 %fusion.9 = f32[640,4608]{1,0:T(8,128)} fusion(bf16[512,4608]{1,0:T(8,128)(2,1)} %all-gather.5.cloned.1.call-done, f32[512,640]{1,0:T(8,128)S(1)} %get-tuple-element.16, s32[640]{0:T(1024)S(1)} %iota_add_fusion, f32[512]{0:T(512)S(1)} %get-tuple-element.14, s32[512]{0:T(512)S(1)} %copy-done), kind=kOutput, calls=%fused_computation.16 | convolution fusion | flops 3022848000 | bytes 17832448 | tf_op jit(solution)/shard_map/tv,td->vd/dot_general | solution.py:34
  256.0 0.0 copy-start.2
  256.0 32.3 %reduce-scatter.5.cloned.1.call-done = bf16[512,288]{0,1:T(8,128)(2,1)} async-done(((bf16[512,4608]{0,1:T(8,128)(2,1)}), bf16[512,288]{0,1:T(8,128)(2,1)}) %reduce-scatter.5.cloned.1.call-update) | async-done | bytes 294928 | tf_op jit(solution)/shard_map/reduce_scatter | solution.py:39
  288.3 2.0 copy.15
  290.3 0.0 reduce-scatter.7.cloned.1.call-update
  290.3 0.6 dynamic_slice.3
  290.9 106.2 %all-gather.7.cloned.1.call-done = bf16[512,4608]{1,0:T(8,128)(2,1)} async-done(((bf16[32,4608]{1,0:T(8,128)(2,1)}), bf16[512,4608]{1,0:T(8,128)(2,1)}) %all-gather.7.cloned.1.call-update) | async-done | bytes 4718608 | tf_op jit(solution)/shard_map/all_gather | solution.py:16
  397.1 0.0 copy-done.2
  397.1 9.3 %add_convert_fusion = bf16[640,4608]{1,0:T(8,128)(2,1)} fusion(f32[640,4608]{1,0:T(8,128)} %fusion.9, bf16[512,4608]{1,0:T(8,128)(2,1)} %all-gather.7.cloned.1.call-done, s32[512]{0:T(512)S(1)} %copy-done.2, s32[640]{0:T(1024)S(1)} %iota_add_fusion), kind=kOutput, calls=%fused_computation | convolution fusion | flops 3029073920 | bytes 22417920 | tf_op jit(solution)/shard_map/dot_general | solution.py:36
  406.3 196.3 %reduce-scatter.7.cloned.1.call-done = f32[32,288]{1,0:T(8,128)} async-done(((f32[512,288]{1,0:T(8,128)}), f32[32,288]{1,0:T(8,128)}) %reduce-scatter.7.cloned.1.call-update) | async-done | bytes 36880
  (2 shorter events, 0.0 us)
Async XLA Ops:
  7.2 126.1 %copy-start = (s32[512]{0:T(512)S(1)}, s32[512]{0:T(512)}, u32[]{:S(2)}) copy-start(s32[512]{0:T(512)} %param.7) | copy-start | bytes 6148
  7.2 126.1 %all-gather.5.cloned.1.call-start = ((), (), s32[]{:S(2)}) async-start(), calls=%async_computation.2 | async-start | bytes 5013504 | tf_op jit(solution)/shard_map/all_gather | solution.py:15
  27.9 260.3 %reduce-scatter.5.cloned.1.call-start = ((), (), s32[]{:S(2)}) async-start(), calls=%async_computation.4 | async-start | bytes 5013504 | tf_op jit(solution)/shard_map/reduce_scatter | solution.py:39
  223.6 0.7 copy-start.1
  223.6 173.4 %all-gather.7.cloned.1.call-start = ((), (), s32[]{:S(2)}) async-start(), calls=%async_computation.3 | async-start | bytes 5013504 | tf_op jit(solution)/shard_map/all_gather | solution.py:16
  245.6 357.1 %reduce-scatter.7.cloned.1.call-start = ((), (), s32[]{:S(2)}) async-start(), calls=%async_computation.5 | async-start | bytes 835584
  256.0 141.1 %copy-start.2 = (s32[512]{0:T(512)S(1)}, s32[512]{0:T(512)}, u32[]{:S(2)}) copy-start(s32[512]{0:T(512)} %param.8) | copy-start | bytes 6148
Sparse Core Ops, SparseCore 0:
  28.0 105.1 all-gather.4
  223.8 64.4 reduce-scatter.4
  290.9 106.1 all-gather.6
  401.3 201.2 reduce-scatter.6
where the time goes:
time: 610 us; the launch traced here: 609 us
  waiting for transfers between devices  440 us (72%)
  blocking collectives  112 us (18%)
  matrix products  37 us (6%)
  between operations  13.8 us (2%)
    unnamed x5, waiting for transfers between devices  196 us
    all_gather x1, waiting for transfers between devices, local(): lax.all_gather(whole_c, 'pipe', axis=0, tiled=True)  106 us
    all_gather x1, waiting for transfers between devices, local(): lax.all_gather(whole_h, 'pipe', axis=0, tiled=True)  105 us
    psum x1, blocking collectives, local(): lax.psum((local_sum, local_target), ('pipe', 'vocab'))  72.8 us
    reduce_scatter x1, waiting for transfers between devices, local(): lax.psum_scatter(products.astype(jnp.bfloat16), 'vocab', scatter_dimensio...  32.3 us
    all_gather x1, blocking collectives, local(): lax.all_gather(embed_cot, 'vocab', axis=1, tiled=True)  19.9 us
    all_gather x1, blocking collectives, local(): lax.all_gather(final_hidden, 'vocab', axis=1, tiled=True)  19.4 us
  transfers between devices with their start and end apart: 4, of which 4 were waited for; matrix products, arithmetic and copies ran while one was open for 4% of the time, Pallas kernels for 0%

commit v1 on v0

--- a/solution.py
+++ b/solution.py
@@ -13,7 +13,9 @@
     )
     whole_h, whole_c = (
         lax.all_gather(whole_h, "pipe", axis=0, tiled=True),
-        lax.all_gather(whole_c, "pipe", axis=0, tiled=True),
+        jnp.concatenate(
+            lax.all_to_all(jnp.stack([whole_c] * lax.axis_size("pipe")), "pipe", 0, 0), axis=0
+        ),
     )
     rows_dev = tied_table.shape[0]
     offset = lax.axis_index(("pipe", "vocab")) * rows_dev

time: 610 us -> 545 us (0.89)
  waiting for transfers between devices: 440 us -> 368 us
    all_gather x1 -> x0, waiting for transfers between devices: 106 us -> none  [local(): lax.all_gather(whole_c, 'pipe', axis=0, tiled=True)]
    all_to_all x0 -> x1, waiting for transfers between devices: none -> 65.5 us  [local(): lax.all_to_all(jnp.stack([whole_c] * lax.axis_size('pipe')), 'pipe', 0, 0)]
    unnamed x5 -> x4, waiting for transfers between devices: 196 us -> 166 us
  transfers between devices with their start and end apart: 4 -> 4, of which waited for: 4 -> 4; matrix products, arithmetic and copies ran while one was open for 4% -> 5% of each run, Pallas kernels for 0% -> 0%
where the time goes in v1:
time: 545 us; the launch traced here: 544 us
  waiting for transfers between devices  368 us (68%)
  blocking collectives  112 us (21%)
  matrix products  37.1 us (7%)
  between operations  13.8 us (3%)
  local copies, waits for them, and re-layouts  7.71 us (1%)
    unnamed x4, waiting for transfers between devices  166 us
    all_gather x1, waiting for transfers between devices, local(): lax.all_gather(whole_h, 'pipe', axis=0, tiled=True)  105 us
    psum x1, blocking collectives, local(): lax.psum((local_sum, local_target), ('pipe', 'vocab'))  72.8 us
    all_to_all x1, waiting for transfers between devices, local(): lax.all_to_all(jnp.stack([whole_c] * lax.axis_size('pipe')), 'pipe', 0, 0)  65.5 us
    reduce_scatter x1, waiting for transfers between devices, local(): lax.psum_scatter(products.astype(jnp.bfloat16), 'vocab', scatter_dimensio...  31.1 us
    all_gather x1, blocking collectives, local(): lax.all_gather(embed_cot, 'vocab', axis=1, tiled=True)  20 us
    all_gather x1, blocking collectives, local(): lax.all_gather(final_hidden, 'vocab', axis=1, tiled=True)  19.4 us
  transfers between devices with their start and end apart: 4, of which 4 were waited for; matrix products, arithmetic and copies ran while one was open for 5% of the time, Pallas kernels for 0%

profile of v1, /device:TPU:2, one launch (start us, length us, event | category | flops | bytes accessed | tf_op | source)
XLA Modules:
  0.0 544.3 jit_solution(8950974292373036436)
XLA Ops:
  7.2 0.0 copy-start
  7.2 0.0 all-gather.4.cloned.1.call-start
  7.2 19.4 %all-gather = bf16[16,288,32]{1,2,0:T(8,128)(2,1)S(1)} all-gather(bf16[1,288,32]{1,2,0:T(8,128)(2,1)} %bitcast.21), channel_id=1, replica_groups=mesh['pipe'=16,'vocab'=16] {'vocab'}, dimensions={0}, use_global_device_ids=true | all-gather | bytes 313344 | tf_op jit(solution)/shard_map/all_gather | solution.py:11
  26.7 0.1 copy.13
  26.8 1.1 reshape.24
  27.9 0.0 all-gather.4.cloned.1.call-update
  27.9 0.0 reduce-scatter.5.cloned.1.call-start
  28.0 105.3 %all-gather.4.cloned.1.call-done = bf16[512,4608]{1,0:T(8,128)(2,1)} async-done(((bf16[32,4608]{1,0:T(8,128)(2,1)}), bf16[512,4608]{1,0:T(8,128)(2,1)}) %all-gather.4.cloned.1.call-update) | async-done | bytes 4718608 | tf_op jit(solution)/shard_map/all_gather | solution.py:15
  133.3 0.0 copy-done
  133.3 7.8 %fusion.4 = (f32[512]{0:T(512)S(1)}, f32[512]{0:T(512)S(1)}, f32[512,640]{1,0:T(8,128)S(1)}) fusion(s32[640]{0:T(1024)S(1)} %iota_add_fusion, s32[512]{0:T(512)S(1)} %copy-done, bf16[512,4608]{1,0:T(8,128)(2,1)} %all-gather.4.cloned.1.call-done, bf16[640,4608]{1,0:T(8,128)(2,1)} %param.6), kind=kOutput, calls=%fused_computation.9 | convolution fusion | flops 3021863936 | bytes 11936256 | tf_op jit(solution)/shard_map/td,vd->tv/dot_general | solution.py:23
  141.0 72.8 %all-reduce = (f32[512]{0:T(512)S(1)}, f32[512]{0:T(512)S(1)}) all-reduce(f32[512]{0:T(512)S(1)} %get-tuple-element.13, f32[512]{0:T(512)S(1)} %get-tuple-element.12), channel_id=1, replica_groups=mesh['pipe'=16,'vocab'=16] {'pipe','vocab'}, use_global_device_ids=true, to_apply=%region_1.2 | all-reduce | flops 1024 | bytes 8192 | tf_op jit(solution)/shard_map/psum | solution.py:30
  213.9 9.9 %convolution_convert_fusion = bf16[512,4608]{0,1:T(8,128)(2,1)} fusion(bf16[640,4608]{1,0:T(8,128)(2,1)} %param.6, f32[512,640]{1,0:T(8,128)S(1)} %get-tuple-element.16, s32[640]{0:T(1024)S(1)} %iota_add_fusion, f32[512]{0:T(512)S(1)} %get-tuple-element.14, s32[512]{0:T(512)S(1)} %copy-done), kind=kOutput, calls=%fused_computation.1 | convolution fusion | flops 3025207296 | bytes 11934208 | tf_op jit(solution)/shard_map/dot_general | solution.py:40
  223.8 0.0 copy-start.1
  223.8 0.0 reduce-scatter.5.cloned.1.call-update
  223.8 0.7 copy-done.1
  224.5 20.0 %all-gather.1 = bf16[16,288,32]{1,2,0:T(8,128)(2,1)S(1)} all-gather(bf16[1,288,32]{1,2,0:T(8,128)(2,1)S(1)} %bitcast.22), channel_id=1, replica_groups=mesh['pipe'=16,'vocab'=16] {'vocab'}, dimensions={0}, use_global_device_ids=true | all-gather | bytes 313344 | tf_op jit(solution)/shard_map/all_gather | solution.py:12
  244.5 0.1 copy.14
  244.6 0.4 reshape.26
  245.0 2.6 stack.2
  247.6 4.9 all-to-all-start
  252.6 0.2 reduce-scatter.7.cloned.1.call-start
  252.8 10.2 %fusion.9 = f32[640,4608]{1,0:T(8,128)} fusion(bf16[512,4608]{1,0:T(8,128)(2,1)} %all-gather.4.cloned.1.call-done, f32[512,640]{1,0:T(8,128)S(1)} %get-tuple-element.16, s32[640]{0:T(1024)S(1)} %iota_add_fusion, f32[512]{0:T(512)S(1)} %get-tuple-element.14, s32[512]{0:T(512)S(1)} %copy-done), kind=kOutput, calls=%fused_computation.16 | convolution fusion | flops 3022848000 | bytes 17832448 | tf_op jit(solution)/shard_map/tv,td->vd/dot_general | solution.py:36
  263.0 0.0 copy-start.2
  263.0 31.1 %reduce-scatter.5.cloned.1.call-done = bf16[512,288]{0,1:T(8,128)(2,1)} async-done(((bf16[512,4608]{0,1:T(8,128)(2,1)}), bf16[512,288]{0,1:T(8,128)(2,1)}) %reduce-scatter.5.cloned.1.call-update) | async-done | bytes 294928 | tf_op jit(solution)/shard_map/reduce_scatter | solution.py:41
  294.1 2.0 copy.16
  296.1 0.0 reduce-scatter.7.cloned.1.call-update
  296.2 0.6 dynamic_slice.3
  296.8 65.5 %all-to-all-done = bf16[16,32,4608]{2,1,0:T(8,128)(2,1)} async-done(((bf16[16,32,4608]{2,1,0:T(8,128)(2,1)}), bf16[16,32,4608]{2,1,0:T(8,128)(2,1)}, u32[]{:S(2)}, u32[]{:S(2)}) %all-to-all-start) | async-done | bytes 4718624 | tf_op jit(solution)/shard_map/all_to_all | solution.py:17
  362.3 0.0 copy-done.2
  362.3 9.3 %add_convert_fusion = bf16[640,4608]{1,0:T(8,128)(2,1)} fusion(f32[640,4608]{1,0:T(8,128)} %fusion.9, bf16[512,4608]{1,0:T(8,128)(2,1)} %bitcast.6, s32[512]{0:T(512)S(1)} %copy-done.2, s32[640]{0:T(1024)S(1)} %iota_add_fusion), kind=kOutput, calls=%fused_computation | convolution fusion | flops 3029073920 | bytes 22417920 | tf_op jit(solution)/shard_map/dot_general | solution.py:38
  371.6 166.2 %reduce-scatter.7.cloned.1.call-done = f32[32,288]{1,0:T(8,128)} async-done(((f32[512,288]{1,0:T(8,128)}), f32[32,288]{1,0:T(8,128)}) %reduce-scatter.7.cloned.1.call-update) | async-done | bytes 36880
  (2 shorter events, 0.0 us)
Async XLA Ops:
  7.2 126.1 %copy-start = (s32[512]{0:T(512)S(1)}, s32[512]{0:T(512)}, u32[]{:S(2)}) copy-start(s32[512]{0:T(512)} %param.7) | copy-start | bytes 6148
  7.2 126.1 %all-gather.4.cloned.1.call-start = ((), (), s32[]{:S(2)}) async-start(), calls=%async_computation.3 | async-start | bytes 5013504 | tf_op jit(solution)/shard_map/all_gather | solution.py:15
  27.9 266.2 %reduce-scatter.5.cloned.1.call-start = ((), (), s32[]{:S(2)}) async-start(), calls=%async_computation.4 | async-start | bytes 5013504 | tf_op jit(solution)/shard_map/reduce_scatter | solution.py:41
  223.8 0.7 copy-start.1
  247.6 114.7 %all-to-all-start = ((bf16[16,32,4608]{2,1,0:T(8,128)(2,1)}), bf16[16,32,4608]{2,1,0:T(8,128)(2,1)}, u32[]{:S(2)}, u32[]{:S(2)}) async-start(bf16[16,32,4608]{2,1,0:T(8,128)(2,1)} %stack.2), calls=%async_computation | async-start | bytes 9437184 | tf_op jit(solution)/shard_map/all_to_all | solution.py:17
  252.6 285.2 %reduce-scatter.7.cloned.1.call-start = ((), (), s32[]{:S(2)}) async-start(), calls=%async_computation.5 | async-start | bytes 835584
  263.0 99.3 %copy-start.2 = (s32[512]{0:T(512)S(1)}, s32[512]{0:T(512)}, u32[]{:S(2)}) copy-start(s32[512]{0:T(512)} %param.8) | copy-start | bytes 6148
Sparse Core Ops, SparseCore 0:
  28.0 105.1 all-gather.3
  223.9 70.1 reduce-scatter.4
  298.5 239.1 reduce-scatter.6
